TPU v7x, 32 devices: a whole 2x2x4 slice. The times are simulated.
32 devices in a mesh: mem: 8 (over z, y), job: 4 (over x, core).
Axes of the slice: x: 2, y: 2, z: 4, core: 2. Of those that a mesh axis runs over, the one named last changes fastest.
Arguments:
- pair_cost: bfloat16 [1536, 128, 128], P(('mem', 'job')), may hold values from -6 to 6
- pair_coef: bfloat16 [1536, 128, 128], P(('mem', 'job')), may hold values from 0.049804688 to 0.5
- slot_member: int32 [32, 48], P(('mem', 'job')), may hold values from 0 to 31, never falling along the last dimension, each value on 1 to 4 neighbouring positions
- slot_owner: int32 [32, 48, 1], P(('mem', 'job')), may hold values from 0 to 7; in each aligned block of 48 rows (0 to 47, 48 to 95, ..., all dimensions but the last counted through in order) at most 9 rows name the same one
- slot_local: int32 [32, 48], P(('mem', 'job')), may hold values from 0 to 15
- duals: float32 [512, 128], P(('mem', 'job')), may hold values from 0.1 to 3
- capacity: int32 [512, 128], P(('mem', 'job')), may hold values from 0 to 39
Outputs:
- primal: bfloat16 [1536, 128, 128], P(('mem', 'job'))
- gradient: float32 [512, 128], P(('mem', 'job'))
- member_share: float32 [256, 128], P('mem')
Inputs may be any that keep to these rules, and one draw needn't show every extreme that they name: `slot_member`: in each device's row the values never fall, every value appears, none more than 4 times, and one exactly 4 times. `slot_owner`: among the 48 entries of one device no value appears more than 9 times, and in some devices one appears exactly 9 times.
All inputs are finite; a program needn't handle non-finite values.
Results may differ from a plain program's by a relative error of at most 0.001.
Values sent between devices are 32-bit elements; how exact they have to be, the bound alone decides.
A program may use at most 64 MiB of HBM per device.

v0:
```python
import jax
import jax.numpy as jnp
from jax import lax
from jax.sharding import PartitionSpec as P

MB_DEV = 32
RIDGE = 1.0


def allocate(pair_cost, pair_coef, dual_rows):
    reduced = pair_cost.astype(jnp.float32) + pair_coef.astype(jnp.float32) * dual_rows[:, None, :]
    allocation = jnp.clip(-reduced / RIDGE, 0.0, 1.0)
    column_part = jnp.sum(pair_coef.astype(jnp.float32) * allocation, axis=1)
    row_part = jnp.sum(allocation, axis=2)
    return (allocation.astype(jnp.bfloat16), column_part, row_part)


def per_device(pair_cost, pair_coef, slot_member, slot_owner, slot_local, duals, capacity):
    slot_count = pair_cost.shape[0]
    block_size = pair_cost.shape[1]
    job_blocks = duals.shape[0]
    mem_count = lax.axis_size("mem")
    owner_index = slot_owner[0, :, 0]
    local_index = slot_local[0]
    peer_slots = max(2, (3 * slot_count + 2 * mem_count - 1) // (2 * mem_count))
    owner_table = (owner_index[:, None] == jnp.arange(mem_count, dtype=jnp.int32)[None, :]).astype(
        jnp.int32
    )
    slot_rank = jnp.sum((jnp.cumsum(owner_table, axis=0) - owner_table) * owner_table, axis=1)
    position = owner_index * peer_slots + slot_rank
    requests = jnp.zeros((mem_count * peer_slots,), jnp.int32).at[position].set(local_index)
    requests = requests.reshape(mem_count, peer_slots)
    received = lax.all_to_all(requests, "mem", split_axis=0, concat_axis=0, tiled=True)
    replies = duals[received]
    fetched, received = (
        lax.all_to_all(replies, "mem", split_axis=0, concat_axis=0, tiled=True),
        received,
    )
    dual_rows = fetched.reshape(mem_count * peer_slots, block_size)[position]
    primal, column_part, row_part = allocate(pair_cost, pair_coef, dual_rows)
    outgoing = (
        jnp.zeros((mem_count * peer_slots, block_size), jnp.float32).at[position].set(column_part)
    )
    incoming = lax.all_to_all(
        outgoing.reshape(mem_count, peer_slots, block_size),
        "mem",
        split_axis=0,
        concat_axis=0,
        tiled=True,
    )
    totals = jax.ops.segment_sum(
        incoming.reshape(mem_count * peer_slots, block_size),
        received.reshape(-1),
        num_segments=job_blocks,
    )
    gradient = totals - capacity.astype(jnp.float32)
    member_table = (jnp.arange(MB_DEV, dtype=jnp.int32)[:, None] == slot_member[0][None, :]).astype(
        jnp.float32
    )
    member_part = jnp.dot(
        member_table, row_part, precision=lax.Precision.HIGHEST, preferred_element_type=jnp.float32
    )
    member_share = lax.psum(member_part, "job") / block_size
    return (primal, gradient, member_share)


def solution(mesh):
    placed = (
        P(("mem", "job"), None, None),
        P(("mem", "job"), None, None),
        P(("mem", "job"), None),
        P(("mem", "job"), None, None),
        P(("mem", "job"), None),
        P(("mem", "job"), None),
        P(("mem", "job"), None),
    )
    return jax.shard_map(
        per_device,
        mesh=mesh,
        in_specs=placed,
        out_specs=(P(("mem", "job"), None, None), P(("mem", "job"), None), P("mem", None)),
        check_vma=False,
    )
```

profile of v0, /device:TPU:0, one launch (start us, length us, event | category | flops | bytes accessed | tf_op | source)
XLA Modules:
  0.0 57.0 jit_solution(11159333356886695551)
XLA Ops:
  0.6 0.7 %fusion.6 = s32[48,8]{1,0:T(8,128)S(1)} fusion(s32[48]{0:T(128)} %bitcast.20), kind=kLoop, calls=%fused_computation.15 | loop fusion | flops 768 | bytes 1728 | tf_op jit(solution)/shard_map/convert_element_type | solution.py:26
  1.5 0.8 %select_reduce_fusion = s32[48]{0:T(128)S(1)} fusion(s32[48,8]{1,0:T(8,128)S(1)} %reduce_window_sum.11, s32[48]{0:T(128)} %bitcast.21), kind=kLoop, calls=%fused_computation.13 | loop fusion | flops 1872 | bytes 1920 | tf_op jit(solution)/shard_map/reduce_sum | solution.py:29
  2.3 0.7 %fusion.13 = s32[48]{0:T(128)S(1)} fusion(s32[48]{0:T(128)S(1)} %select_reduce_fusion, s32[1,48,1]{1,2,0:T(1,128)} %param.10), kind=kLoop, calls=%fused_computation.29 | loop fusion | flops 240 | bytes 576 | tf_op jit(solution)/shard_map/select_n | solution.py:31
  3.0 0.9 %scatter_custom_fusion = s32[72]{0:T(128)S(1)} fusion(s32[48]{0:T(128)S(1)} %fusion.13, s32[48]{0:T(128)} %bitcast.23, s32[]{:T(128)} %constant.8.clone.1), kind=kCustom, calls=%fused_computation.31 | custom fusion | bytes 800 | tf_op jit(solution)/shard_map/scatter | solution.py:31
  3.9 13.6 %all_to_all.22 = s32[8,1,9]{2,1,0:T(1,128)S(1)} all-to-all(s32[8,1,9]{2,1,0:T(1,128)S(1)} %bitcast.19), channel_id=1, replica_groups=mesh['mem'=8,'job'=4] {'mem'}, dimensions={0} | all-to-all | bytes 576 | tf_op jit(solution)/shard_map/all_to_all | solution.py:33
  17.5 0.1 reshape.83
  17.6 0.6 %gather_fusion = f32[72,128]{1,0:T(8,128)S(1)} fusion(f32[16,128]{1,0:T(8,128)S(1)} %copy-done, s32[1024]{0:T(1024)S(1)} %pad_clamp_fusion.1), kind=kCustom, calls=%fused_computation | custom fusion | bytes 74016 | tf_op jit(solution)/shard_map/gather | solution.py:34
  18.2 0.6 %reshape.82 = f32[8,9,128]{2,1,0:T(8,128)} reshape(f32[72,128]{1,0:T(8,128)S(1)} %gather_fusion) | data formatting | bytes 73728 | tf_op jit(solution)/shard_map/gather | solution.py:34
  18.8 3.4 %all-to-all-start.1 = ((f32[8,9,128]{2,1,0:T(8,128)}), f32[8,9,128]{2,1,0:T(8,128)S(1)}, u32[]{:S(2)}, u32[]{:S(2)}) async-start(f32[8,9,128]{2,1,0:T(8,128)} %reshape.82), calls=%async_computation.1 | async-start | bytes 131072 | tf_op jit(solution)/shard_map/all_to_all | solution.py:36
  22.2 0.5 broadcast.65
  22.7 0.7 %reduce.3 = s32[8,9]{1,0:T(8,128)S(1)} reduce(s32[8,1,9]{2,1,0:T(1,128)S(1)} %all_to_all.22, s32[]{:T(128)} %broadcast.65), dimensions={1}, to_apply=%all_to_all.15.reduce_sub_computation.3 | reduce | bytes 580 | tf_op jit(solution)/shard_map/all_to_all | solution.py:33
  23.4 0.1 reshape.115
  23.5 5.6 %all-to-all-done.1 = f32[8,9,128]{2,1,0:T(8,128)S(1)} async-done(((f32[8,9,128]{2,1,0:T(8,128)}), f32[8,9,128]{2,1,0:T(8,128)S(1)}, u32[]{:S(2)}, u32[]{:S(2)}) %all-to-all-start.1) | async-done | bytes 36896 | tf_op jit(solution)/shard_map/all_to_all | solution.py:36
  29.0 0.6 %gather_fusion.1 = f32[48,128]{1,0:T(8,128)S(1)} fusion(f32[72,128]{1,0:T(8,128)S(1)} %reshape.78, s32[1024]{0:T(1024)S(1)} %pad_clamp_fusion), kind=kCustom, calls=%fused_computation.1 | custom fusion | bytes 49344 | tf_op jit(solution)/shard_map/gather | solution.py:39
  29.6 4.1 %fusion.4 = (f32[48,128]{1,0:T(8,128)S(1)}, f32[48,128]{1,0:T(8,128)S(1)}, bf16[48,128,128]{2,1,0:T(8,128)(2,1)}) fusion(bf16[48,128,128]{2,1,0:T(8,128)(2,1)} %param.8, bf16[48,128,128]{2,1,0:T(8,128)(2,1)} %param.7, f32[48,128]{1,0:T(8,128)S(1)} %gather_fusion.1), kind=kLoop, calls=%fused_computation.11 | loop fusion | flops 7852032 | bytes 4792320 | tf_op jit(solution)/shard_map/reduce_sum | solution.py:14
  33.8 0.1 fusion.9
  33.9 10.1 %psum.7 = f32[32,128]{1,0:T(8,128)S(1)} all-reduce(f32[32,128]{1,0:T(8,128)S(1)} %fusion.9), channel_id=1, replica_groups=mesh['mem'=8,'job'=4] {'job'}, use_global_device_ids=true, to_apply=%region_7.8 | all-reduce | flops 4096 | bytes 32768 | tf_op jit(solution)/shard_map/psum | solution.py:63
  44.0 0.7 %scatter_custom_fusion.1 = f32[72,128]{1,0:T(8,128)S(1)} fusion(s32[48]{0:T(128)S(1)} %fusion.13, f32[48,128]{1,0:T(8,128)S(1)} %get-tuple-element.4, f32[]{:T(128)} %constant.7.clone.1), kind=kCustom, calls=%fused_computation.16 | custom fusion | bytes 36868 | tf_op jit(solution)/shard_map/scatter | solution.py:42
  44.7 0.6 %reshape.79 = f32[8,9,128]{2,1,0:T(8,128)} reshape(f32[72,128]{1,0:T(8,128)S(1)} %scatter_custom_fusion.1) | data formatting | bytes 73728 | tf_op jit(solution)/shard_map/reshape | solution.py:45
  45.3 3.3 %all-to-all-start.2 = ((f32[8,9,128]{2,1,0:T(8,128)}), f32[8,9,128]{2,1,0:T(8,128)S(1)}, u32[]{:S(2)}, u32[]{:S(2)}) async-start(f32[8,9,128]{2,1,0:T(8,128)} %reshape.79), calls=%async_computation.2 | async-start | bytes 131072 | tf_op jit(solution)/shard_map/all_to_all | solution.py:44
  48.7 0.6 %broadcast_multiply_fusion = f32[32,128]{1,0:T(8,128)} fusion(f32[32,128]{1,0:T(8,128)S(1)} %psum.7), kind=kLoop, calls=%fused_computation.21 | loop fusion | flops 4096 | bytes 32768 | tf_op jit(solution)/shard_map/div | solution.py:63
  49.3 6.2 %all-to-all-done.2 = f32[8,9,128]{2,1,0:T(8,128)S(1)} async-done(((f32[8,9,128]{2,1,0:T(8,128)}), f32[8,9,128]{2,1,0:T(8,128)S(1)}, u32[]{:S(2)}, u32[]{:S(2)}) %all-to-all-start.2) | async-done | bytes 36896 | tf_op jit(solution)/shard_map/all_to_all | solution.py:44
  55.5 0.8 %scatter_custom_fusion.2 = f32[16,128]{1,0:T(8,128)S(1)} fusion(s32[72]{0:T(128)S(1)} %reshape.115, f32[72,128]{1,0:T(8,128)S(1)} %reshape.117, f32[]{:T(128)} %constant.7.clone.1), kind=kCustom, calls=%fused_computation.26 | custom fusion | flops 9216 | bytes 8196 | tf_op jit(solution)/shard_map/scatter-add | solution.py:51
  56.3 0.6 %convert_subtract_fusion = f32[16,128]{1,0:T(8,128)} fusion(f32[16,128]{1,0:T(8,128)S(1)} %scatter_custom_fusion.2, s32[16,128]{1,0:T(8,128)S(1)} %copy-done.1), kind=kLoop, calls=%fused_computation.23 | loop fusion | flops 4096 | bytes 24576 | tf_op jit(solution)/shard_map/sub | solution.py:56
  (13 shorter events, 0.2 us)
Async XLA Ops:
  0.6 17.0 %copy-start = (f32[16,128]{1,0:T(8,128)S(1)}, f32[16,128]{1,0:T(8,128)}, u32[]{:S(2)}) copy-start(f32[16,128]{1,0:T(8,128)} %param.12) | copy-start | bytes 24580
  18.8 10.2 %all-to-all-start.1 = ((f32[8,9,128]{2,1,0:T(8,128)}), f32[8,9,128]{2,1,0:T(8,128)S(1)}, u32[]{:S(2)}, u32[]{:S(2)}) async-start(f32[8,9,128]{2,1,0:T(8,128)} %reshape.82), calls=%async_computation.1 | async-start | bytes 131072 | tf_op jit(solution)/shard_map/all_to_all | solution.py:36
  29.6 4.1 %copy-start.2 = (s32[1,48]{1,0:T(1,128)S(1)}, s32[1,48]{1,0:T(1,128)}, u32[]{:S(2)}) copy-start(s32[1,48]{1,0:T(1,128)} %param.9) | copy-start | bytes 580
  29.6 26.7 %copy-start.1 = (s32[16,128]{1,0:T(8,128)S(1)}, s32[16,128]{1,0:T(8,128)}, u32[]{:S(2)}) copy-start(s32[16,128]{1,0:T(8,128)} %param.13) | copy-start | bytes 24580
  45.3 10.2 %all-to-all-start.2 = ((f32[8,9,128]{2,1,0:T(8,128)}), f32[8,9,128]{2,1,0:T(8,128)S(1)}, u32[]{:S(2)}, u32[]{:S(2)}) async-start(f32[8,9,128]{2,1,0:T(8,128)} %reshape.79), calls=%async_computation.2 | async-start | bytes 131072 | tf_op jit(solution)/shard_map/all_to_all | solution.py:44
where the time goes:
time: 57.4 us; the launch traced here: 57 us
  blocking collectives  23.7 us (41%)
  waiting for transfers between devices  11.8 us (21%)
  other arithmetic  9.12 us (16%)
  starting transfers between devices  6.7 us (12%)
  local copies, waits for them, and re-layouts  4.76 us (8%)
  between operations  0.73 us (1%)
    all_to_all x1, blocking collectives, per_device(): lax.all_to_all(requests, 'mem', split_axis=0, concat_axis=0, tiled=True)  13.6 us
    psum x1, blocking collectives, per_device(): member_share = lax.psum(member_part, 'job') / block_size  10.1 us
    all_to_all x1, waiting for transfers between devices, per_device(): lax.all_to_all(outgoing.reshape(mem_count, peer_slots, block_size), 'mem'...  6.23 us
    all_to_all x1, waiting for transfers between devices, per_device(): lax.all_to_all(replies, 'mem', split_axis=0, concat_axis=0, tiled=True)  5.57 us
    reduce_sum x1, other arithmetic, allocate(): row_part = jnp.sum(allocation, axis=2)  4.11 us
    all_to_all x1, starting transfers between devices, per_device(): lax.all_to_all(replies, 'mem', split_axis=0, concat_axis=0, tiled=True)  3.35 us
    all_to_all x1, starting transfers between devices, per_device(): lax.all_to_all(outgoing.reshape(mem_count, peer_slots, block_size), 'mem'...  3.35 us
    gather x2, local copies, waits for them, and re-layouts, per_device(): replies = duals[received]  1.24 us
  transfers between devices with their start and end apart: 2, of which 2 were waited for; matrix products, arithmetic and copies ran while one was open for 3% of the time, Pallas kernels for 0%

commit v1 on v0

--- a/solution.py
+++ b/solution.py
@@ -5,6 +5,30 @@
 
 MB_DEV = 32
 RIDGE = 1.0
+
+
+def split_up(shard, dim, size):
+    lengths = shard.shape
+    pieces = shard.reshape(*lengths[:dim], size, lengths[dim] // size, *lengths[dim + 1 :])
+    return jnp.moveaxis(pieces, dim, 0)
+
+
+def joined_along(blocks, dim):
+    lengths = list(blocks.shape[1:])
+    lengths[dim] *= blocks.shape[0]
+    return jnp.moveaxis(blocks, 0, dim).reshape(lengths)
+
+
+def sent_to_each(value, axis, split_dim, concat_dim):
+    devices, index = (lax.axis_size(axis), lax.axis_index(axis))
+    tiles = split_up(value, split_dim, devices)
+    whole = tiles
+    for step in range(1, devices):
+        target, source = ((index + step) % devices, (index - step) % devices)
+        sent = lax.dynamic_index_in_dim(tiles, target, 0)
+        theirs = lax.ppermute(sent, axis, [(i, (i + step) % devices) for i in range(devices)])
+        whole = lax.dynamic_update_slice_in_dim(whole, theirs, source, axis=0)
+    return joined_along(whole, concat_dim)
 
 
 def allocate(pair_cost, pair_coef, dual_rows):
@@ -32,10 +56,7 @@
     requests = requests.reshape(mem_count, peer_slots)
     received = lax.all_to_all(requests, "mem", split_axis=0, concat_axis=0, tiled=True)
     replies = duals[received]
-    fetched, received = (
-        lax.all_to_all(replies, "mem", split_axis=0, concat_axis=0, tiled=True),
-        received,
-    )
+    fetched, received = (sent_to_each(replies, "mem", 0, 0), received)
     dual_rows = fetched.reshape(mem_count * peer_slots, block_size)[position]
     primal, column_part, row_part = allocate(pair_cost, pair_coef, dual_rows)
     outgoing = (

time: 57.4 us -> 65.7 us (1.14)
  blocking collectives: 23.7 us -> 10.1 us
  starting transfers between devices: 6.7 us -> 19.9 us
  waiting for transfers between devices: 11.8 us -> 20.8 us
    all_to_all x1 -> x0, blocking collectives: 13.6 us -> none  [per_device(): lax.all_to_all(requests, 'mem', split_axis=0, concat_axis=0, tiled=True)]
    ppermute x0 -> x7, starting transfers between devices: none -> 8.58 us  [sent_to_each(): lax.ppermute(sent, axis, [(i, (i + step) % devices) for i in range(device...]
    ppermute x0 -> x7, waiting for transfers between devices: none -> 8.19 us  [sent_to_each(): lax.ppermute(sent, axis, [(i, (i + step) % devices) for i in range(device...]
    all_to_all x1, starting transfers between devices: 3.35 us -> 7.31 us  [per_device(): lax.all_to_all(requests, 'mem', split_axis=0, concat_axis=0, tiled=True)]
    all_to_all x1, waiting for transfers between devices: 5.57 us -> 6.36 us  [per_device(): lax.all_to_all(requests, 'mem', split_axis=0, concat_axis=0, tiled=True)]
  transfers between devices with their start and end apart: 2 -> 9, of which waited for: 2 -> 4; matrix products, arithmetic and copies ran while one was open for 3% -> 3% of each run, Pallas kernels for 0% -> 0%
where the time goes in v1:
time: 65.7 us; the launch traced here: 65.3 us
  waiting for transfers between devices  20.8 us (32%)
  starting transfers between devices  19.9 us (30%)
  blocking collectives  10.1 us (15%)
  other arithmetic  8.76 us (13%)
  local copies, waits for them, and re-layouts  4.79 us (7%)
  between operations  0.82 us (1%)
    psum x1, blocking collectives, per_device(): member_share = lax.psum(member_part, 'job') / block_size  10.1 us
    ppermute x7, starting transfers between devices, sent_to_each(): lax.ppermute(sent, axis, [(i, (i + step) % devices) for i in range(device...  8.58 us
    ppermute x7, waiting for transfers between devices, sent_to_each(): lax.ppermute(sent, axis, [(i, (i + step) % devices) for i in range(device...  8.19 us
    all_to_all x1, starting transfers between devices, per_device(): lax.all_to_all(requests, 'mem', split_axis=0, concat_axis=0, tiled=True)  7.31 us
    all_to_all x1, waiting for transfers between devices, per_device(): lax.all_to_all(requests, 'mem', split_axis=0, concat_axis=0, tiled=True)  6.36 us
    all_to_all x1, waiting for transfers between devices, per_device(): lax.all_to_all(outgoing.reshape(mem_count, peer_slots, block_size), 'mem'...  6.3 us
    all_to_all x1, starting transfers between devices, per_device(): lax.all_to_all(outgoing.reshape(mem_count, peer_slots, block_size), 'mem'...  3.98 us
    reduce_sum x1, other arithmetic, allocate(): row_part = jnp.sum(allocation, axis=2)  3.63 us
  transfers between devices with their start and end apart: 9, of which 4 were waited for; matrix products, arithmetic and copies ran while one was open for 3% of the time, Pallas kernels for 0%

profile of v1, /device:TPU:0, one launch (start us, length us, event | category | flops | bytes accessed | tf_op | source)
XLA Modules:
  0.0 65.3 jit_solution(16654476113410152033)
XLA Ops:
  0.7 0.8 %fusion.6 = s32[48,8]{1,0:T(8,128)S(1)} fusion(s32[48]{0:T(128)} %bitcast.35), kind=kLoop, calls=%fused_computation.15 | loop fusion | flops 768 | bytes 1728 | tf_op jit(solution)/shard_map/convert_element_type | solution.py:50
  1.6 0.8 %select_reduce_fusion = s32[48]{0:T(128)S(1)} fusion(s32[48,8]{1,0:T(8,128)S(1)} %reduce_window_sum.11, s32[48]{0:T(128)} %bitcast.36), kind=kLoop, calls=%fused_computation.13 | loop fusion | flops 1872 | bytes 1920 | tf_op jit(solution)/shard_map/reduce_sum | solution.py:53
  2.4 0.7 %fusion.13 = s32[48]{0:T(128)S(1)} fusion(s32[48]{0:T(128)S(1)} %select_reduce_fusion, s32[1,48,1]{1,2,0:T(1,128)} %param.10), kind=kLoop, calls=%fused_computation.43 | loop fusion | flops 240 | bytes 576 | tf_op jit(solution)/shard_map/select_n | solution.py:55
  3.1 0.9 %scatter_custom_fusion = s32[72]{0:T(128)S(1)} fusion(s32[48]{0:T(128)S(1)} %fusion.13, s32[48]{0:T(128)} %bitcast.38, s32[]{:T(128)} %constant.115.clone.1), kind=kCustom, calls=%fused_computation.45 | custom fusion | bytes 800 | tf_op jit(solution)/shard_map/scatter | solution.py:55
  3.9 0.7 %all_to_all.11 = s32[8,1,9]{2,0,1:T(8,128)} reshape(s32[72]{0:T(128)S(1)} %scatter_custom_fusion) | data formatting | bytes 576 | tf_op jit(solution)/shard_map/all_to_all | solution.py:57
  4.6 7.3 %all-to-all-start = ((s32[8,1,9]{2,1,0:T(1,128)}), s32[8,1,9]{2,1,0:T(1,128)S(1)}, u32[]{:S(2)}, u32[]{:S(2)}) async-start(s32[8,1,9]{2,1,0:T(1,128)} %bitcast.5), calls=%async_computation | async-start | bytes 8192 | tf_op jit(solution)/shard_map/all_to_all | solution.py:57
  12.0 6.4 %all-to-all-done = s32[8,1,9]{2,1,0:T(1,128)S(1)} async-done(((s32[8,1,9]{2,1,0:T(1,128)}), s32[8,1,9]{2,1,0:T(1,128)S(1)}, u32[]{:S(2)}, u32[]{:S(2)}) %all-to-all-start) | async-done | bytes 320 | tf_op jit(solution)/shard_map/all_to_all | solution.py:57
  18.4 0.6 gather_fusion
  19.1 0.6 collective-permute-start
  20.2 0.7 %reduce.3 = s32[8,9]{1,0:T(8,128)S(1)} reduce(s32[8,1,9]{2,1,0:T(1,128)S(1)} %all-to-all-done, s32[]{:T(128)} %broadcast.79), dimensions={1}, to_apply=%all_to_all.12.reduce_sub_computation.3 | reduce | bytes 580 | tf_op jit(solution)/shard_map/all_to_all | solution.py:57
  21.0 4.2 %collective-permute-start.6 = (f32[1,1,9,128]{3,2,0,1:T(8,128)S(1)}, f32[1,1,9,128]{3,2,0,1:T(8,128)S(1)}, u32[]{:S(2)}, u32[]{:S(2)}) collective-permute-start(f32[1,1,9,128]{3,2,0,1:T(8,128)S(1)} %get-tuple-element.6), channel_id=1, source_target_pairs={{0,28},{4,0},{8,4},{12,8},{16,12},{20,16},{24,20},{28,24},{1,29},{... | collective-permute-start | bytes 13832 | tf_op jit(solution)/shard_map/ppermute | solution.py:29
  25.4 2.7 %collective-permute-start.2 = (f32[1,1,9,128]{3,2,0,1:T(8,128)S(1)}, f32[1,1,9,128]{3,2,0,1:T(8,128)S(1)}, u32[]{:S(2)}, u32[]{:S(2)}) collective-permute-start(f32[1,1,9,128]{3,2,0,1:T(8,128)S(1)} %get-tuple-element.9), channel_id=1, source_target_pairs={{0,12},{4,16},{8,20},{12,24},{16,28},{20,0},{24,4},{28,8},{1,13},{... | collective-permute-start | bytes 13832 | tf_op jit(solution)/shard_map/ppermute | solution.py:29
  28.3 5.2 %collective-permute-done.1 = f32[1,1,9,128]{3,2,0,1:T(8,128)S(1)} collective-permute-done((f32[1,1,9,128]{3,2,0,1:T(8,128)S(1)}, f32[1,1,9,128]{3,2,0,1:T(8,128)S(1)}, u32[]{:S(2)}, u32[]{:S(2)}) %collective-permute-start.1) | collective-permute-done | bytes 4640 | tf_op jit(solution)/shard_map/ppermute | solution.py:29
  33.5 0.6 collective-permute-start.5
  34.2 3.0 %collective-permute-done.5 = f32[1,1,9,128]{3,2,0,1:T(8,128)S(1)} collective-permute-done((f32[1,1,9,128]{3,2,0,1:T(8,128)S(1)}, f32[1,1,9,128]{3,2,0,1:T(8,128)S(1)}, u32[]{:S(2)}, u32[]{:S(2)}) %collective-permute-start.5) | collective-permute-done | bytes 4640 | tf_op jit(solution)/shard_map/ppermute | solution.py:29
  37.8 3.6 %fusion.4 = (f32[48,128]{1,0:T(8,128)S(1)}, f32[48,128]{1,0:T(8,128)S(1)}, bf16[48,128,128]{2,1,0:T(8,128)(2,1)}) fusion(bf16[48,128,128]{2,1,0:T(8,128)(2,1)S(1)} %copy-done.1, bf16[48,128,128]{2,1,0:T(8,128)(2,1)} %param.7, f32[48,128]{1,0:T(8,128)S(1)} %gather_fusion.1), kind=kLoop, calls=%fused_computation.11 | loop fusion | flops 7852032 | bytes 4792320 | tf_op jit(solution)/shard_map/reduce_sum | solution.py:38
  41.6 10.1 %psum.7 = f32[32,128]{1,0:T(8,128)S(1)} all-reduce(f32[32,128]{1,0:T(8,128)S(1)} %fusion.9), channel_id=1, replica_groups=mesh['mem'=8,'job'=4] {'job'}, use_global_device_ids=true, to_apply=%region_7.8 | all-reduce | flops 4096 | bytes 32768 | tf_op jit(solution)/shard_map/psum | solution.py:84
  51.7 0.7 %scatter_custom_fusion.1 = f32[72,128]{1,0:T(8,128)S(1)} fusion(s32[48]{0:T(128)S(1)} %fusion.13, f32[48,128]{1,0:T(8,128)S(1)} %get-tuple-element.4, f32[]{:T(128)} %constant.114.clone.1), kind=kCustom, calls=%fused_computation.16 | custom fusion | bytes 36868 | tf_op jit(solution)/shard_map/scatter | solution.py:63
  52.4 0.6 reshape.86
  53.0 4.0 %all-to-all-start.1 = ((f32[8,9,128]{2,1,0:T(8,128)}), f32[8,9,128]{2,1,0:T(8,128)S(1)}, u32[]{:S(2)}, u32[]{:S(2)}) async-start(f32[8,9,128]{2,1,0:T(8,128)} %reshape.86), calls=%async_computation.1 | async-start | bytes 131072 | tf_op jit(solution)/shard_map/all_to_all | solution.py:65
  57.0 0.6 broadcast_multiply_fusion
  57.6 6.3 %all-to-all-done.1 = f32[8,9,128]{2,1,0:T(8,128)S(1)} async-done(((f32[8,9,128]{2,1,0:T(8,128)}), f32[8,9,128]{2,1,0:T(8,128)S(1)}, u32[]{:S(2)}, u32[]{:S(2)}) %all-to-all-start.1) | async-done | bytes 36896 | tf_op jit(solution)/shard_map/all_to_all | solution.py:65
  63.9 0.8 %scatter_custom_fusion.2 = f32[16,128]{1,0:T(8,128)S(1)} fusion(s32[72]{0:T(128)S(1)} %reshape.122, f32[72,128]{1,0:T(8,128)S(1)} %reshape.124, f32[]{:T(128)} %constant.114.clone.1), kind=kCustom, calls=%fused_computation.33 | custom fusion | flops 9216 | bytes 8196 | tf_op jit(solution)/shard_map/scatter-add | solution.py:72
  64.7 0.6 convert_subtract_fusion
  (37 shorter events, 2.0 us)
Async XLA Ops:
  0.6 17.8 %copy-start = (f32[16,128]{1,0:T(8,128)S(1)}, f32[16,128]{1,0:T(8,128)}, u32[]{:S(2)}) copy-start(f32[16,128]{1,0:T(8,128)} %param.12) | copy-start | bytes 24580
  0.6 37.1 %copy-start.1 = (bf16[48,128,128]{2,1,0:T(8,128)(2,1)S(1)}, bf16[48,128,128]{2,1,0:T(8,128)(2,1)}, u32[]{:S(2)}) copy-start(bf16[48,128,128]{2,1,0:T(8,128)(2,1)} %param.8) | copy-start | bytes 4718596
  4.6 13.7 %all-to-all-start = ((s32[8,1,9]{2,1,0:T(1,128)}), s32[8,1,9]{2,1,0:T(1,128)S(1)}, u32[]{:S(2)}, u32[]{:S(2)}) async-start(s32[8,1,9]{2,1,0:T(1,128)} %bitcast.5), calls=%async_computation | async-start | bytes 8192 | tf_op jit(solution)/shard_map/all_to_all | solution.py:57
  19.1 9.0 %collective-permute-start = (f32[1,1,9,128]{3,2,0,1:T(8,128)S(1)}, f32[1,1,9,128]{3,2,0,1:T(8,128)S(1)}, u32[]{:S(2)}, u32[]{:S(2)}) collective-permute-start(f32[1,1,9,128]{3,2,0,1:T(8,128)S(1)} %get-tuple-element.11), channel_id=1, source_target_pairs={{0,4},{4,8},{8,12},{12,16},{16,20},{20,24},{24,28},{28,0},{1,5},{5... | collective-permute-start | bytes 13832 | tf_op jit(solution)/shard_map/ppermute | solution.py:29
  21.0 16.2 %collective-permute-start.6 = (f32[1,1,9,128]{3,2,0,1:T(8,128)S(1)}, f32[1,1,9,128]{3,2,0,1:T(8,128)S(1)}, u32[]{:S(2)}, u32[]{:S(2)}) collective-permute-start(f32[1,1,9,128]{3,2,0,1:T(8,128)S(1)} %get-tuple-element.6), channel_id=1, source_target_pairs={{0,28},{4,0},{8,4},{12,8},{16,12},{20,16},{24,20},{28,24},{1,29},{... | collective-permute-start | bytes 13832 | tf_op jit(solution)/shard_map/ppermute | solution.py:29
  25.1 9.1 %collective-permute-start.4 = (f32[1,1,9,128]{3,2,0,1:T(8,128)S(1)}, f32[1,1,9,128]{3,2,0,1:T(8,128)S(1)}, u32[]{:S(2)}, u32[]{:S(2)}) collective-permute-start(f32[1,1,9,128]{3,2,0,1:T(8,128)S(1)} %get-tuple-element.7), channel_id=1, source_target_pairs={{0,20},{4,24},{8,28},{12,0},{16,4},{20,8},{24,12},{28,16},{1,21},{... | collective-permute-start | bytes 13832 | tf_op jit(solution)/shard_map/ppermute | solution.py:29
  25.1 9.0 %collective-permute-start.3 = (f32[1,1,9,128]{3,2,0,1:T(8,128)S(1)}, f32[1,1,9,128]{3,2,0,1:T(8,128)S(1)}, u32[]{:S(2)}, u32[]{:S(2)}) collective-permute-start(f32[1,1,9,128]{3,2,0,1:T(8,128)S(1)} %get-tuple-element.8), channel_id=1, source_target_pairs={{0,16},{4,20},{8,24},{12,28},{16,0},{20,4},{24,8},{28,12},{1,17},{... | collective-permute-start | bytes 13832 | tf_op jit(solution)/shard_map/ppermute | solution.py:29
  25.4 8.8 %collective-permute-start.2 = (f32[1,1,9,128]{3,2,0,1:T(8,128)S(1)}, f32[1,1,9,128]{3,2,0,1:T(8,128)S(1)}, u32[]{:S(2)}, u32[]{:S(2)}) collective-permute-start(f32[1,1,9,128]{3,2,0,1:T(8,128)S(1)} %get-tuple-element.9), channel_id=1, source_target_pairs={{0,12},{4,16},{8,20},{12,24},{16,28},{20,0},{24,4},{28,8},{1,13},{... | collective-permute-start | bytes 13832 | tf_op jit(solution)/shard_map/ppermute | solution.py:29
  28.1 5.4 %collective-permute-start.1 = (f32[1,1,9,128]{3,2,0,1:T(8,128)S(1)}, f32[1,1,9,128]{3,2,0,1:T(8,128)S(1)}, u32[]{:S(2)}, u32[]{:S(2)}) collective-permute-start(f32[1,1,9,128]{3,2,0,1:T(8,128)S(1)} %get-tuple-element.10), channel_id=1, source_target_pairs={{0,8},{4,12},{8,16},{12,20},{16,24},{20,28},{24,0},{28,4},{1,9},{5... | collective-permute-start | bytes 13832 | tf_op jit(solution)/shard_map/ppermute | solution.py:29
  33.5 3.7 %collective-permute-start.5 = (f32[1,1,9,128]{3,2,0,1:T(8,128)S(1)}, f32[1,1,9,128]{3,2,0,1:T(8,128)S(1)}, u32[]{:S(2)}, u32[]{:S(2)}) collective-permute-start(f32[1,1,9,128]{3,2,0,1:T(8,128)S(1)} %get-tuple-element.12), channel_id=1, source_target_pairs={{0,24},{4,28},{8,0},{12,4},{16,8},{20,12},{24,16},{28,20},{1,25},{... | collective-permute-start | bytes 13832 | tf_op jit(solution)/shard_map/ppermute | solution.py:29
  37.8 3.7 %copy-start.3 = (s32[1,48]{1,0:T(1,128)S(1)}, s32[1,48]{1,0:T(1,128)}, u32[]{:S(2)}) copy-start(s32[1,48]{1,0:T(1,128)} %param.9) | copy-start | bytes 580
  37.8 26.9 %copy-start.2 = (s32[16,128]{1,0:T(8,128)S(1)}, s32[16,128]{1,0:T(8,128)}, u32[]{:S(2)}) copy-start(s32[16,128]{1,0:T(8,128)} %param.13) | copy-start | bytes 24580
  53.0 10.9 %all-to-all-start.1 = ((f32[8,9,128]{2,1,0:T(8,128)}), f32[8,9,128]{2,1,0:T(8,128)S(1)}, u32[]{:S(2)}, u32[]{:S(2)}) async-start(f32[8,9,128]{2,1,0:T(8,128)} %reshape.86), calls=%async_computation.1 | async-start | bytes 131072 | tf_op jit(solution)/shard_map/all_to_all | solution.py:65
